TPU v7x, 256 devices: a whole 4x4x8 slice. The times are simulated.
256 devices in a mesh: tm: 32 (over y, x, core), space: 8 (over z).
Axes of the slice: x: 4, y: 4, z: 8, core: 2. Of those that a mesh axis runs over, the one named last changes fastest.
Arguments:
- latent_tokens: bfloat16 [64, 1792, 2240], P('tm', 'space'), may hold values from -6 to 6
- norm_gain: float32 [2240], replicated, may hold values from 0.5 to 1.5
- w_query: bfloat16 [2240, 1120], P('tm', 'space'), may hold values from -0.125 to 0.125
- w_key: bfloat16 [2240, 1120], P('tm', 'space'), may hold values from -0.125 to 0.125
- w_value: bfloat16 [2240, 1120], P('tm', 'space'), may hold values from -0.125 to 0.125
- out_gain: float32 [1120], replicated, may hold values from 0.5 to 1.5
- block_ids: int32 [64], P('tm'), may hold values from 0 to 15, never falling along the last dimension, each value on 1 to 8 neighbouring positions
Outputs:
- attended: bfloat16 [64, 1792, 1120], P('tm', 'space')
Inputs may be any that keep to these rules, and one draw needn't show every extreme that they name: `block_ids`: block numbers never fall from one frame to the next; each of the 16 blocks holds 1 to 8 frames and one holds exactly 8.
All inputs are finite; a program needn't handle non-finite values.
Results may differ from a plain program's by a relative error of at most 0.0065.
Values may be sent and summed in bfloat16 or wider, within the bound.
A program may use at most 192 MiB of HBM per device.

v0:
```python
import jax
import jax.numpy as jnp
from jax import lax
from jax.sharding import PartitionSpec as P

HEAD = 112
HEADS = 10


def prefix(value, axis, join, neutral):
    count, mine = (lax.axis_size(axis), lax.axis_index(axis))
    pieces = lax.all_gather(value, axis)
    so_far = jnp.full_like(value, 0) + jnp.asarray(neutral, value.dtype)

    def step(position, so_far):
        longer = join(so_far, pieces[position])
        return jnp.where(position < mine, longer, so_far)

    return lax.fori_loop(0, count - 1, step, so_far)


def carried_in(x, axis, join, neutral):
    count = lax.axis_size(axis)
    place = lax.axis_index(axis)
    ahead = count - 1 - place
    gathered = jax.tree.map(
        lambda a, kind: lax.all_gather(a.astype(kind), axis),
        x,
        jax.tree.map(lambda a: jnp.bfloat16 if a.dtype == jnp.float32 else a.dtype, x),
    )
    state = jax.tree.map(lambda a, e: jnp.zeros_like(a) + jnp.asarray(e, a.dtype), x, neutral)

    def one(step, state):
        source = count - 1 - step
        return join(
            state,
            jax.tree.map(
                lambda a, own: lax.dynamic_index_in_dim(a, source, 0, False).astype(own.dtype),
                gathered,
                x,
            ),
        )

    return lax.fori_loop(0, ahead, one, state)


def add_states(earlier, later):
    return earlier + later


def join_later(earlier, later):
    high_vacant, high_leading, high_uniform, high_running = earlier
    low_vacant, low_leading, low_uniform, low_running = later
    matching = (high_leading == low_leading).astype(jnp.float32)
    joined = low_uniform * matching * (1.0 - high_vacant)
    low_absent = low_vacant > 0.5
    leading = jnp.where(low_absent, high_leading, low_leading)
    vacant = low_vacant * high_vacant
    uniform = jnp.where(
        low_absent,
        high_uniform,
        low_uniform * (high_vacant + (1.0 - high_vacant) * high_uniform * matching),
    )
    running = jnp.where(low_absent, high_running, low_running + joined * high_running)
    return (vacant, leading, uniform, running)


def on_device(latent_tokens, norm_gain, w_query, w_key, w_value, out_gain, block_ids):
    frame_count, token_count, width = latent_tokens.shape
    row_count = frame_count * token_count
    values = latent_tokens.reshape(row_count, width).astype(jnp.float32)
    meansq = jnp.mean(values * values, axis=-1, keepdims=True)
    normed = (values * lax.rsqrt(meansq + 1e-06) * norm_gain).astype(jnp.bfloat16)
    stacked = jnp.stack((w_query, w_key, w_value))
    columns_full = lax.all_gather(stacked, "space", axis=2, tiled=True)
    projected = jnp.einsum(
        "rn,cnh->crh",
        normed,
        lax.all_gather(columns_full, "tm", axis=1, tiled=True),
        preferred_element_type=jnp.float32,
    )
    channels = projected.shape[2]
    query = jax.nn.relu(projected[0]).reshape(frame_count, token_count, HEADS, HEAD)
    key = (
        jax.nn.relu(projected[1])
        .astype(jnp.bfloat16)
        .reshape(frame_count, token_count, HEADS, HEAD)
    )
    value = projected[2].astype(jnp.bfloat16).reshape(frame_count, token_count, HEADS, HEAD)
    local_states = jnp.einsum("fthk,fthv->fhkv", key, value, preferred_element_type=jnp.float32)
    per_frame_state = lax.psum(local_states, "space")
    device_sum = jnp.sum(per_frame_state, axis=0)
    zero_state = jnp.zeros_like(device_sum)
    before = prefix(device_sum, "tm", add_states, zero_state)
    leading_id = block_ids[0]
    closing_id = block_ids[frame_count - 1]
    within_leading = (block_ids == leading_id).astype(jnp.float32)
    leading_sum = jnp.einsum(
        "o,owpe->wpe", within_leading, per_frame_state, precision=lax.Precision.HIGHEST
    )
    uniform_flag = jnp.min(within_leading)
    leading_float = leading_id.astype(jnp.float32)
    closing_float = closing_id.astype(jnp.float32)
    summary = (jnp.float32(0.0), leading_float, uniform_flag, leading_sum)
    identity = (jnp.float32(1.0), jnp.float32(0.0), jnp.float32(1.0), zero_state)
    vacant, leading, uniform, running = carried_in(summary, "tm", join_later, identity)
    reaches = (1.0 - vacant) * (leading == closing_float).astype(jnp.float32)
    trailing = reaches * running
    earlier_mask = (block_ids[None, :] <= block_ids[:, None]).astype(jnp.float32)
    in_closing = (block_ids == closing_id).astype(jnp.float32)
    carried = before[None] + jnp.einsum(
        "ij,jhkv->ihkv", earlier_mask, per_frame_state, precision=lax.Precision.HIGHEST
    )
    carried = carried + in_closing[:, None, None, None] * trailing[None]
    numerator = jnp.einsum("fthk,fhkv->fthv", query, carried, precision=lax.Precision.HIGHEST)
    head_meansq = jnp.mean(numerator * numerator, axis=-1, keepdims=True)
    result = numerator * lax.rsqrt(head_meansq + 1e-06) * out_gain.reshape(HEADS, HEAD)
    return result.reshape(frame_count, token_count, channels).astype(jnp.bfloat16)


def solution(mesh):
    placed = (
        P("tm", "space", None),
        P(),
        P("tm", "space"),
        P("tm", "space"),
        P("tm", "space"),
        P(),
        P("tm"),
    )
    return jax.shard_map(
        on_device, mesh=mesh, in_specs=placed, out_specs=P("tm", "space", None), check_vma=False
    )
```

profile of v0, /device:TPU:32, one launch (start us, length us, event | category | flops | bytes accessed | tf_op | source)
XLA Modules:
  0.0 544.3 jit_solution(14924308415363143273)
XLA Ops:
  7.7 29.9 %all_gather.33 = bf16[3,70,1120]{1,0,2:T(4,128)(2,1)S(1)} all-gather(bf16[3,70,140]{1,0,2:T(4,128)(2,1)S(1)} %copy.37), channel_id=1, replica_groups=mesh['tm'=32,'space'=8] {'space'}, dimensions={2}, use_global_device_ids=true | all-gather | bytes 529200 | tf_op jit(solution)/shard_map/all_gather | solution.py:75
  37.6 2.2 copy.38
  40.5 1.9 fusion.7
  42.4 84.1 %all-gather.6.cloned.1.call-done = bf16[3,2240,1120]{2,0,1:T(4,128)(2,1)} async-done(((bf16[3,70,1120]{2,0,1:T(4,128)(2,1)}), bf16[3,2240,1120]{2,0,1:T(4,128)(2,1)}) %all-gather.6.cloned.1.call-update) | async-done | bytes 15052816 | tf_op jit(solution)/shard_map/all_gather | solution.py:79
  126.5 14.1 %fusion.3 = f32[3,448,1120]{2,1,0:T(8,128)S(1)} fusion(bf16[3,2240,1120]{2,0,1:T(4,128)(2,1)} %all-gather.6.cloned.1.call-done, bf16[448,2240]{1,0:T(8,128)(2,1)} %fusion.7), kind=kOutput, calls=%fused_computation.5 | convolution fusion | flops 6743654400 | bytes 23080960 | tf_op jit(solution)/shard_map/rn,cnh->crh/dot_general | solution.py:76
  140.7 1.4 fusion.13
  142.1 1.5 copy-done.2
  143.6 3.4 reshape.84
  147.0 3.1 reshape.83
  150.1 3.1 fusion.16
  153.9 75.4 %all-reduce.6.cloned.1.call-done = f32[2,10,112,112]{3,2,1,0:T(8,128)} async-done(((f32[2,10,112,112]{3,2,1,0:T(8,128)}), f32[2,10,112,112]{3,2,1,0:T(8,128)}) %all-reduce.6.cloned.1.call-update) | async-done | bytes 1003536 | tf_op jit(solution)/shard_map/psum | solution.py:91
  229.3 4.7 fusion.20
  239.7 1.3 dynamic-update-slice.2
  241.0 63.4 %all-reduce.3 = (bf16[32]{0:T(256)(128)(2,1)S(1)}, bf16[32]{0:T(256)(128)(2,1)S(1)}, bf16[32]{0:T(256)(128)(2,1)S(1)}) all-reduce(bf16[32]{0:T(256)(128)(2,1)S(1)} %dynamic-update-slice, bf16[32]{0:T(256)(128)(2,1)S(1)} %dynamic-update-slice.1, bf16[32]{0:T(256)(128)(2,1)S(1)} %dynamic-update-slice.2), channel_id=1, replica_groups=mesh['tm'=32,'space'=8] {'tm'}, use_global_device_ids=true, to_apply=%add | all-reduce | flops 96 | bytes 384
  305.6 1.7 slice_maximum_fusion
  307.4 3.3 reshape.85
  310.7 177.9 %while.32 = (s32[]{:T(128)}, f32[]{:T(128)}, f32[]{:T(128)}, f32[10,112,112]{2,1,0:T(8,128)S(1)}, s32[]{:T(128)}, /*index=5*/bf16[32]{0:T(256)(128)(2,1)S(1)}, b...) while((s32[]{:T(128)}, f32[]{:T(128)}, f32[]{:T(128)}, ...), condition=%wide.region_7.8_spmd, body=%wide.region_6.7_spmd.sunk | while | flops 501773 | bytes 1254722 | solution.py:44
  320.9 1.3 fusion.33
  361.1 1.3 fusion.33
  488.6 38.9 %while.33 = (s32[]{:T(128)}, f32[10,112,112]{2,1,0:T(8,128)S(1)}, s32[]{:T(128)}, f32[32,10,112,112]{3,2,1,0:T(8,128)}, s32[]{:T(128)}, /*index=5*/s32[]{:T(128)}) while((s32[]{:T(128)}, f32[10,112,112]{2,1,0:T(8,128)S(1)}, s32[]{:T(128)}, f32[32,10,112,112]{3,2,1,0:T(8,128)}, s32[]{:T(128)}, /*index=5*/s32[]{:T(128)}) %tuple.73), condition=%wide.region_4.5_spmd.clone, body=%wide.region_3.4_spmd.clone.sunk | while | flops 376324 | bytes 1505381 | solution.py:19
  488.6 1.3 add_select_fusion.2
  527.6 3.3 fusion.15
  530.9 5.1 fusion.8
  536.4 1.4 copy.48
  (201 shorter events, 133.8 us)
Async XLA Ops:
  6.5 120.0 %all-gather.6.cloned.1.call-start = ((), (), s32[]{:S(2)}) async-start(), calls=%async_computation | async-start | bytes 21288960 | tf_op jit(solution)/shard_map/all_gather | solution.py:79
  6.5 33.4 %copy-start.1 = (bf16[2,224,2240]{2,1,0:T(8,128)(2,1)S(1)}, bf16[2,224,2240]{2,1,0:T(8,128)(2,1)}, u32[]{:S(2)}) copy-start(bf16[2,224,2240]{2,1,0:T(8,128)(2,1)} %param.11) | copy-start | bytes 6021124
  37.6 2.9 copy-start.5
  39.9 189.4 %all-reduce.6.cloned.1.call-start = ((), (), s32[]{:S(2)}) async-start(), calls=%async_computation.1 | async-start | bytes 2293760 | tf_op jit(solution)/shard_map/psum | solution.py:91
  140.7 2.9 copy-start.2
  150.1 3.2 copy-start.7
  153.3 157.4 %all-gather.10.cloned.1.call-start = ((), (), s32[]{:S(2)}) async-start(), calls=%async_computation.3 | async-start | bytes 9461760 | tf_op jit(solution)/shard_map/all_gather | solution.py:27
  229.3 5.6 %copy-start.3 = (f32[2,10,112,112]{3,2,1,0:T(8,128)S(1)}, f32[2,10,112,112]{3,2,1,0:T(8,128)}, u32[]{:S(2)}) copy-start(f32[2,10,112,112]{3,2,1,0:T(8,128)} %all-reduce.6.cloned.1.call-done) | copy-start | bytes 3010564
  234.0 2.5 copy-start.8
  234.0 71.0 %copy-start.6 = (f32[1120]{0:T(1024)S(1)}, f32[1120]{0:T(1024)}, u32[]{:S(2)}) copy-start(f32[1120]{0:T(1024)} %param.16) | copy-start | bytes 13444
  234.8 253.8 %all-gather.8.cloned.1.call-start = ((), (), s32[]{:S(2)}) async-start(), calls=%async_computation.2 | async-start | bytes 18923520 | tf_op jit(solution)/shard_map/all_gather | solution.py:12
  488.6 38.9 %copy-start.4 = (f32[2,10,112,112]{3,2,1,0:T(8,128)S(1)}, f32[2,10,112,112]{3,2,1,0:T(8,128)}, u32[]{:S(2)}) copy-start(f32[2,10,112,112]{3,2,1,0:T(8,128)} %all-reduce.6.cloned.1.call-done) | copy-start | bytes 3010564
  527.6 3.3 copy-start
Sparse Core Ops, SparseCore 0:
  40.0 86.5 all-gather.5
  153.4 75.8 all-reduce.5
  235.0 58.7 all-gather.9
  296.1 80.6 all-gather.7
where the time goes:
time: 548 us; the launch traced here: 544 us
  waiting for transfers between devices  160 us (29%)
  blocking collectives  93.3 us (17%)
  loops' own time  87.7 us (16%)
  other arithmetic  87.5 us (16%)
  local copies, waits for them, and re-layouts  71.2 us (13%)
  matrix products  30.4 us (6%)
  between operations  14.5 us (3%)
    another operation x1, loops' own time, carried_in(): return lax.fori_loop(0, ahead, one, state)  86.9 us
    all_gather x1, waiting for transfers between devices, on_device(): lax.all_gather(columns_full, 'tm', axis=1, tiled=True)  84.1 us
    psum x1, waiting for transfers between devices, on_device(): per_frame_state = lax.psum(local_states, 'space')  75.4 us
    unnamed x1, blocking collectives  63.4 us
    dynamic_slice x93, local copies, waits for them, and re-layouts, one(): lax.dynamic_index_in_dim(a, source, 0, False).astype(own.dtype)  52 us
    select_n x31, other arithmetic, join_later(): jnp.where(low_absent, high_running, low_running + joined * high_running)  38.9 us
    select_n x31, other arithmetic, step(): return jnp.where(position < mine, longer, so_far)  38.2 us
    all_gather x1, blocking collectives, on_device(): columns_full = lax.all_gather(stacked, 'space', axis=2, tiled=True)  29.9 us
  transfers between devices with their start and end apart: 4, of which 2 were waited for; matrix products, arithmetic and copies ran while one was open for 19% of the time, Pallas kernels for 0%

commit v1 on v0

--- a/solution.py
+++ b/solution.py
@@ -5,6 +5,9 @@
 
 HEAD = 112
 HEADS = 10
+step_on_skins_in = lambda s0, mesh_ax: jnp.concatenate(
+    lax.all_to_all(jnp.stack([s0] * lax.psum(1, mesh_ax), axis=0), mesh_ax, 0, 0), axis=1
+)
 
 
 def prefix(value, axis, join, neutral):
@@ -76,7 +79,7 @@
     projected = jnp.einsum(
         "rn,cnh->crh",
         normed,
-        lax.all_gather(columns_full, "tm", axis=1, tiled=True),
+        step_on_skins_in(columns_full, "tm"),
         preferred_element_type=jnp.float32,
     )
     channels = projected.shape[2]

time: 548 us -> 713 us (1.30)
  waiting for transfers between devices: 160 us -> 271 us
  local copies, waits for them, and re-layouts: 71.2 us -> 115 us
  starting transfers between devices: 0.13 us -> 7.69 us
    all_to_all x0 -> x1, waiting for transfers between devices: none -> 200 us  [lax.all_to_all(jnp.stack([s0] * lax.psum(1, mesh_ax), axis=0), mesh_ax, 0...]
    all_gather x1 -> x0, waiting for transfers between devices: 84.1 us -> none  [on_device(): lax.all_gather(columns_full, 'tm', axis=1, tiled=True)]
    reshape x0 -> x2, local copies, waits for them, and re-layouts: none -> 34.8 us  [jnp.concatenate(lax.all_to_all(jnp.stack([s0] * lax.psum(1, mesh_ax), axi...]
    all_to_all x0 -> x1, starting transfers between devices: none -> 7.57 us  [lax.all_to_all(jnp.stack([s0] * lax.psum(1, mesh_ax), axis=0), mesh_ax, 0...]
  transfers between devices with their start and end apart: 4 -> 4, of which waited for: 2 -> 2; matrix products, arithmetic and copies ran while one was open for 19% -> 15% of each run, Pallas kernels for 0% -> 0%
where the time goes in v1:
time: 713 us; the launch traced here: 708 us
  waiting for transfers between devices  271 us (38%)
  local copies, waits for them, and re-layouts  115 us (16%)
  loops' own time  93.6 us (13%)
  blocking collectives  93.3 us (13%)
  other arithmetic  85.8 us (12%)
  matrix products  27.2 us (4%)
  between operations  14.6 us (2%)
  starting transfers between devices  7.69 us (1%)
    all_to_all x1, waiting for transfers between devices, lax.all_to_all(jnp.stack([s0] * lax.psum(1, mesh_ax), axis=0), mesh_ax, 0...  200 us
    another operation x1, loops' own time, carried_in(): return lax.fori_loop(0, ahead, one, state)  92.8 us
    psum x1, waiting for transfers between devices, on_device(): per_frame_state = lax.psum(local_states, 'space')  70.8 us
    unnamed x1, blocking collectives  63.4 us
    dynamic_slice x93, local copies, waits for them, and re-layouts, one(): lax.dynamic_index_in_dim(a, source, 0, False).astype(own.dtype)  53.8 us
    select_n x31, other arithmetic, join_later(): jnp.where(low_absent, high_running, low_running + joined * high_running)  38.9 us
    select_n x31, other arithmetic, step(): return jnp.where(position < mine, longer, so_far)  38.2 us
    reshape x2, local copies, waits for them, and re-layouts, jnp.concatenate(lax.all_to_all(jnp.stack([s0] * lax.psum(1, mesh_ax), axi...  34.8 us
  transfers between devices with their start and end apart: 4, of which 2 were waited for; matrix products, arithmetic and copies ran while one was open for 15% of the time, Pallas kernels for 0%

profile of v1, /device:TPU:32, one launch (start us, length us, event | category | flops | bytes accessed | tf_op | source)
XLA Modules:
  0.0 708.1 jit_solution(1049333634457209465)
XLA Ops:
  7.6 29.9 %all_gather.30 = bf16[3,70,1120]{1,0,2:T(4,128)(2,1)S(1)} all-gather(bf16[3,70,140]{1,0,2:T(4,128)(2,1)S(1)} %copy.37), channel_id=1, replica_groups=mesh['tm'=32,'space'=8] {'space'}, dimensions={2}, use_global_device_ids=true | all-gather | bytes 529200 | tf_op jit(solution)/shard_map/all_gather | solution.py:78
  37.4 1.4 copy.38
  38.8 5.7 stack.14
  44.6 7.6 %all-to-all-start = ((bf16[32,3,70,1120]{3,2,1,0:T(8,128)(2,1)}), bf16[32,3,70,1120]{3,2,1,0:T(8,128)(2,1)}, u32[]{:S(2)}, u32[]{:S(2)}) async-start(bf16[32,3,70,1120]{3,2,1,0:T(8,128)(2,1)} %stack.14), calls=%async_computation | async-start | bytes 31850496 | tf_op jit(solution)/shard_map/all_to_all | solution.py:9
  54.3 200.4 %all-to-all-done = bf16[32,3,70,1120]{3,2,1,0:T(8,128)(2,1)} async-done(((bf16[32,3,70,1120]{3,2,1,0:T(8,128)(2,1)}), bf16[32,3,70,1120]{3,2,1,0:T(8,128)(2,1)}, u32[]{:S(2)}, u32[]{:S(2)}) %all-to-all-start) | async-done | bytes 15052832 | tf_op jit(solution)/shard_map/all_to_all | solution.py:9
  254.8 13.5 %copy.39 = bf16[3,32,70,1120]{3,2,1,0:T(8,128)(2,1)} copy(bf16[3,32,70,1120]{3,2,0,1:T(8,128)(2,1)} %bitcast.9) | data formatting | bytes 30105600 | tf_op jit(solution)/shard_map/reshape | solution.py:8
  268.3 21.2 %reshape.69 = bf16[3,2240,1120]{2,1,0:T(8,128)(2,1)} reshape(bf16[3,32,70,1120]{3,2,1,0:T(8,128)(2,1)} %copy.39) | data formatting | bytes 30105600 | tf_op jit(solution)/shard_map/reshape | solution.py:8
  289.5 11.0 %convolution_bitcast_fusion = f32[3,448,1120]{2,1,0:T(8,128)S(1)} fusion(bf16[448,2240,1]{1,0,2:T(8,128)(2,1)S(1)} %bitcast.61, bf16[3,2240,1120]{2,1,0:T(8,128)(2,1)} %reshape.69), kind=kOutput, calls=%fused_computation.5 | convolution fusion | flops 6743654400 | bytes 23080960 | tf_op jit(solution)/shard_map/rn,cnh->crh/dot_general | solution.py:79
  300.5 2.6 copy-done
  304.3 3.4 reshape.95
  307.7 3.1 reshape.96
  310.9 3.1 fusion.11
  314.6 70.8 %all-reduce.6.cloned.1.call-done = f32[2,10,112,112]{3,2,1,0:T(8,128)} async-done(((f32[2,10,112,112]{3,2,1,0:T(8,128)}), f32[2,10,112,112]{3,2,1,0:T(8,128)}) %all-reduce.6.cloned.1.call-update) | async-done | bytes 1003536 | tf_op jit(solution)/shard_map/psum | solution.py:94
  385.4 4.7 fusion.15
  395.2 1.3 dynamic-update-slice.2
  397.2 63.4 %all-reduce.3 = (bf16[32]{0:T(256)(128)(2,1)S(1)}, bf16[32]{0:T(256)(128)(2,1)S(1)}, bf16[32]{0:T(256)(128)(2,1)S(1)}) all-reduce(bf16[32]{0:T(256)(128)(2,1)S(1)} %dynamic-update-slice, bf16[32]{0:T(256)(128)(2,1)S(1)} %dynamic-update-slice.1, bf16[32]{0:T(256)(128)(2,1)S(1)} %dynamic-update-slice.2), channel_id=1, replica_groups=mesh['tm'=32,'space'=8] {'tm'}, use_global_device_ids=true, to_apply=%add | all-reduce | flops 96 | bytes 384
  461.8 1.7 slice_maximum_fusion
  463.5 3.3 reshape.97
  466.8 185.5 %while.32 = (s32[]{:T(128)}, f32[]{:T(128)}, f32[]{:T(128)}, f32[10,112,112]{2,1,0:T(8,128)S(1)}, s32[]{:T(128)}, /*index=5*/bf16[32]{0:T(256)(128)(2,1)S(1)}, b...) while((s32[]{:T(128)}, f32[]{:T(128)}, f32[]{:T(128)}, ...), condition=%wide.region_7.8_spmd, body=%wide.region_6.7_spmd.sunk | while | flops 501773 | bytes 1254698 | solution.py:47
  652.5 38.9 %while.33 = (s32[]{:T(128)}, f32[10,112,112]{2,1,0:T(8,128)S(1)}, s32[]{:T(128)}, f32[32,10,112,112]{3,2,1,0:T(8,128)}, s32[]{:T(128)}, /*index=5*/s32[]{:T(128)}) while((s32[]{:T(128)}, f32[10,112,112]{2,1,0:T(8,128)S(1)}, s32[]{:T(128)}, f32[32,10,112,112]{3,2,1,0:T(8,128)}, s32[]{:T(128)}, /*index=5*/s32[]{:T(128)}) %tuple.71), condition=%wide.region_4.5_spmd.clone, body=%wide.region_3.4_spmd.clone.sunk | while | flops 376324 | bytes 1505373 | solution.py:22
  652.5 1.3 add_select_fusion.2
  691.4 3.3 fusion.10
  694.8 5.1 fusion.4
  700.2 1.4 copy.48
  (204 shorter events, 140.7 us)
Async XLA Ops:
  44.6 7.6 %copy-start.2 = (bf16[2,224,2240]{2,1,0:T(8,128)(2,1)S(1)}, bf16[2,224,2240]{2,1,0:T(8,128)(2,1)}, u32[]{:S(2)}) copy-start(bf16[2,224,2240]{2,1,0:T(8,128)(2,1)} %param.11) | copy-start | bytes 6021124
  44.6 8.1 %copy-start.6 = (f32[2240]{0:T(1024)S(1)}, f32[2240]{0:T(1024)}, u32[]{:S(2)}) copy-start(f32[2240]{0:T(1024)} %param.12) | copy-start | bytes 26884
  44.6 210.2 %all-to-all-start = ((bf16[32,3,70,1120]{3,2,1,0:T(8,128)(2,1)}), bf16[32,3,70,1120]{3,2,1,0:T(8,128)(2,1)}, u32[]{:S(2)}, u32[]{:S(2)}) async-start(bf16[32,3,70,1120]{3,2,1,0:T(8,128)(2,1)} %stack.14), calls=%async_computation | async-start | bytes 31850496 | tf_op jit(solution)/shard_map/all_to_all | solution.py:9
  52.1 333.3 %all-reduce.6.cloned.1.call-start = ((), (), s32[]{:S(2)}) async-start(), calls=%async_computation.1 | async-start | bytes 2293760 | tf_op jit(solution)/shard_map/psum | solution.py:94
  52.2 1.6 copy-start.3
  300.5 2.6 copy-start
  310.8 3.2 copy-start.8
  314.0 152.8 %all-gather.7.cloned.1.call-start = ((), (), s32[]{:S(2)}) async-start(), calls=%async_computation.3 | async-start | bytes 9461760 | tf_op jit(solution)/shard_map/all_gather | solution.py:30
  385.4 5.6 copy-start.4
  390.2 2.5 copy-start.9
  390.2 71.0 %copy-start.7 = (f32[1120]{0:T(1024)S(1)}, f32[1120]{0:T(1024)}, u32[]{:S(2)}) copy-start(f32[1120]{0:T(1024)} %param.16) | copy-start | bytes 13444
  391.0 261.5 %all-gather.5.cloned.1.call-start = ((), (), s32[]{:S(2)}) async-start(), calls=%async_computation.2 | async-start | bytes 18923520 | tf_op jit(solution)/shard_map/all_gather | solution.py:15
  652.5 38.9 %copy-start.5 = (f32[2,10,112,112]{3,2,1,0:T(8,128)S(1)}, f32[2,10,112,112]{3,2,1,0:T(8,128)}, u32[]{:S(2)}) copy-start(f32[2,10,112,112]{3,2,1,0:T(8,128)} %all-reduce.6.cloned.1.call-done) | copy-start | bytes 3010564
  691.4 3.3 copy-start.1
Sparse Core Ops, SparseCore 0:
  314.1 71.2 all-reduce.5
  391.1 58.7 all-gather.6
  452.5 80.7 all-gather.4
